TPU v7x, 32 devices: a whole 2x2x4 slice. The times are simulated.
32 devices in a mesh: groups: 2 (over x), stem: 8 (over z, y), cuts: 2 (over core).
Axes of the slice: x: 2, y: 2, z: 4, core: 2. Of those that a mesh axis runs over, the one named last changes fastest.
Arguments:
- stem: bfloat16 [4, 2, 4096, 1024], P(('groups', 'cuts'), None, 'stem'), parts along dimension 0, may hold values from -6 to 6
- edge_values: int32 [4, 4], P(('groups', 'cuts')), parts along dimension 0, may hold values from 0 to 1
- index_order: int32 [1024], replicated, may hold values from 0 to 1023, each once
- branch_first: bfloat16 [2, 1024, 1024], replicated, may hold values from -0.125 to 0.125
- branch_second: bfloat16 [2, 1024, 1024], replicated, may hold values from -0.125 to 0.125
- branch_third: bfloat16 [2, 1024, 256], replicated, may hold values from -0.125 to 0.125
- edge_table: float32 [16, 2, 256], replicated, may hold values from -6 to 6
- picks: int32 [4096], P('stem'), may hold values from 0 to 511, as said below
Outputs:
- amplitudes: float32 [2, 8192, 256], P(None, ('groups', 'stem')), parts along dimension 1
There are 2 independent parts, one for each index of `groups`. A program takes and returns all parts, laid end to end along the dimension named above; an argument that names none is the same for every part. Nothing has to cross between parts.
Inputs may be any that keep to these rules, and one draw needn't show every extreme that they name: `index_order`: each number of 0 to 1023 once. `picks`: each aligned block of 512 entries names every number of 0 to 511 once.
All inputs are finite; a program needn't handle non-finite values.
Results may differ from a plain program's by a relative error of at most 0.0041.
Values may be sent and summed in bfloat16 or wider, within the bound.
No kernel may reach another device: no remote copies, remote signals or barrier semaphores. Data moves between devices by JAX's collectives and lax.ppermute only.
A program may use at most 64 MiB of HBM per device.

v0:
```python
import jax
import jax.numpy as jnp
from jax import lax
from jax.sharding import PartitionSpec as P


def swapped(value, axis, distance):
    mask = 2**distance
    pairs = [(source, source ^ mask) for source in range(lax.axis_size(axis))]
    return lax.ppermute(value, axis, pairs)


def complex_dot(operand, matrix):
    real = jnp.dot(operand[0], matrix[0], preferred_element_type=jnp.float32) - jnp.dot(
        operand[1], matrix[1], preferred_element_type=jnp.float32
    )
    imag = jnp.dot(operand[0], matrix[1], preferred_element_type=jnp.float32) + jnp.dot(
        operand[1], matrix[0], preferred_element_type=jnp.float32
    )
    return jnp.stack([real, imag])


def on_device(
    stem, edge_values, index_order, branch_first, branch_second, branch_third, edge_table, picks
):
    stem_size = lax.axis_size("stem")
    bit_pos = stem_size.bit_length() - 2
    top_bit = lax.axis_index("stem") // (stem_size // 2) % 2
    is_low = top_bit == 0
    width = branch_first.shape[1]
    half_width = width // 2
    rows_dev = stem.shape[2]
    block_rows = rows_dev // stem_size
    inverse = jnp.zeros_like(index_order).at[index_order].set(jnp.arange(width, dtype=jnp.int32))
    reordered = jnp.take(branch_second, inverse, axis=1)
    powers = 2 ** jnp.arange(edge_values.shape[1], dtype=jnp.int32)
    codes = jnp.arange(edge_table.shape[0], dtype=jnp.int32)
    first = complex_dot(stem[0], branch_first).astype(jnp.bfloat16)
    low_half = first[:, :, :half_width]
    high_half = first[:, :, half_width:]
    outgoing = jnp.where(is_low, high_half, low_half)
    incoming = swapped(outgoing, "stem", bit_pos)
    joined = jnp.where(
        is_low,
        jnp.concatenate([low_half, incoming], axis=2),
        jnp.concatenate([incoming, high_half], axis=2),
    )
    second = complex_dot(joined, reordered).astype(jnp.bfloat16)
    contracted = complex_dot(second, branch_third)
    moved = lax.all_to_all(
        contracted.reshape(2, stem_size, block_rows, contracted.shape[2]),
        "stem",
        split_axis=1,
        concat_axis=1,
        tiled=True,
    )
    third = jnp.take(moved.reshape(2, rows_dev, contracted.shape[2]), picks, axis=1)
    code = jnp.sum(edge_values[0] * powers)
    onehot = (codes == code).astype(jnp.float32)
    factor = jnp.sum(onehot[:, None, None] * edge_table, axis=0)
    real = third[0] * factor[0][None, :] - third[1] * factor[1][None, :]
    imag = third[0] * factor[1][None, :] + third[1] * factor[0][None, :]
    total = jnp.stack([real, imag])
    return lax.psum(total, "cuts")


def solution(mesh):
    return jax.shard_map(
        on_device,
        mesh=mesh,
        in_specs=(
            P(("groups", "cuts"), None, "stem", None),
            P(("groups", "cuts"), None),
            P(),
            P(),
            P(),
            P(),
            P(),
            P("stem"),
        ),
        out_specs=P(None, ("groups", "stem"), None),
        check_vma=False,
    )
```

profile of v0, /device:TPU:0, one launch (start us, length us, event | category | flops | bytes accessed | tf_op | source)
XLA Modules:
  0.0 144.1 jit_solution(4913342444032320021)
XLA Ops:
  6.5 0.0 copy-start.4
  6.5 0.0 copy-start.6
  6.5 4.6 %fusion.2 = f32[512,1024]{1,0:T(8,128)} fusion(bf16[2,1024,1024]{2,1,0:T(8,128)(2,1)} %param.11, bf16[1,2,512,1024]{3,2,1,0:T(8,128)(2,1)} %param.8), kind=kOutput, calls=%fused_computation.11 | convolution fusion | flops 1073741824 | bytes 5242880 | tf_op jit(solution)/shard_map/dot_general | solution.py:14
  11.2 0.0 copy-done.4
  11.2 0.0 copy-done.6
  11.2 2.6 %fusion = f32[512,1024]{1,0:T(8,128)} fusion(bf16[2,1024,1024]{2,1,0:T(8,128)(2,1)S(1)} %copy-done.4, bf16[1,2,512,1024]{3,2,1,0:T(8,128)(2,1)S(1)} %copy-done.6), kind=kOutput, calls=%fused_computation.9 | convolution fusion | flops 1073741824 | bytes 5242880 | tf_op jit(solution)/shard_map/dot_general | solution.py:17
  13.8 0.0 copy-start.5
  13.8 0.0 copy-start.8
  13.8 3.6 %fusion.20 = bf16[1,512,1024]{2,1,0:T(8,128)(2,1)S(1)} fusion(f32[512,1024]{1,0:T(8,128)} %fusion.2, bf16[2,1024,1024]{2,1,0:T(8,128)(2,1)} %param.11, bf16[1,2,512,1024]{3,2,1,0:T(8,128)(2,1)S(1)} %copy-done.6), kind=kOutput, calls=%fused_computation.29 | convolution fusion | flops 1074790400 | bytes 6291456 | tf_op jit(solution)/shard_map/dot_general | solution.py:14
  17.4 0.0 copy-done.5
  17.4 0.5 copy-done.8
  17.9 1.3 fusion.23
  19.2 0.0 copy-start.3
  19.2 0.5 broadcast_select_fusion
  19.7 4.1 %collective-permute-start = (bf16[2,512,512]{2,1,0:T(8,128)(2,1)S(1)}, bf16[2,512,512]{2,1,0:T(8,128)(2,1)}, u32[]{:S(2)}, u32[]{:S(2)}) collective-permute-start(bf16[2,512,512]{2,1,0:T(8,128)(2,1)S(1)} %get-tuple-element.5), channel_id=1, source_target_pairs={{0,8},{2,10},{4,12},{6,14},{8,0},{10,2},{12,4},{14,6},{1,9},{3,11}... | collective-permute-start | bytes 3145736 | tf_op jit(solution)/shard_map/ppermute | solution.py:10
  23.8 0.0 copy-done.3
  23.8 4.5 %scatter_custom_fusion = s32[1024]{0:T(1024)S(1)} fusion(s32[1024]{0:T(1024)S(1)} %compare_select_fusion.1, s32[1024]{0:T(1024)S(1)} %iota.11, s32[]{:T(128)} %constant.69.clone.1), kind=kCustom, calls=%fused_computation.69 | custom fusion | bytes 4100 | tf_op jit(solution)/shard_map/scatter | solution.py:34
  28.3 27.6 %gather_fusion = bf16[1024,2,1024]{2,0,1:T(8,128)(2,1)} fusion(bf16[2,1024,1024]{2,1,0:T(8,128)(2,1)} %param.12, s32[1024]{0:T(1024)S(1)} %fusion.46), kind=kCustom, calls=%fused_computation | custom fusion | bytes 8392704 | tf_op jit(solution)/shard_map/jit(_take)/gather | solution.py:35
  56.0 2.6 %select_bitcast_fusion = bf16[2,1024,1024]{2,1,0:T(8,128)(2,1)S(1)} fusion(bf16[1024,2,1024]{2,0,1:T(8,128)(2,1)} %gather_fusion, pred[1024]{0:T(1024)(128)(4,1)S(1)} %compare_and_fusion), kind=kLoop, calls=%fused_computation.3 | loop fusion | flops 2097152 | bytes 8389632 | tf_op jit(solution)/shard_map/jit(_take)/select_n | solution.py:35
  58.6 10.9 %collective-permute-done = bf16[2,512,512]{2,1,0:T(8,128)(2,1)} collective-permute-done((bf16[2,512,512]{2,1,0:T(8,128)(2,1)S(1)}, bf16[2,512,512]{2,1,0:T(8,128)(2,1)}, u32[]{:S(2)}, u32[]{:S(2)}) %collective-permute-start) | collective-permute-done | bytes 1048608 | tf_op jit(solution)/shard_map/ppermute | solution.py:10
  69.6 2.2 %maximum_select_fusion = bf16[2,512,1024]{2,1,0:T(8,128)(2,1)S(1)} fusion(bf16[2,512,512]{2,1,0:T(8,128)(2,1)} %collective-permute-done, bf16[2,512,512]{2,1,0:T(8,128)(2,1)S(1)} %get-tuple-element.6, bf16[2,512,512]{2,1,0:T(8,128)(2,1)S(1)} %get-tuple-element.7, pred[]{:T(512)S(6)} %eq.15), kind=kLoop, calls=%fused_computation.8 | loop fusion | flops 9437184 | bytes 5242881 | tf_op jit(solution)/shard_map/jit(_where)/select_n | solution.py:43
  71.8 1.3 fusion.8
  73.1 1.3 fusion.11
  74.3 0.0 copy-start
  74.3 1.3 subtract_convert_fusion
  75.6 0.0 copy-done
  75.6 0.4 fusion.40
  76.1 0.5 fusion.36
  76.6 1.3 add_convert_fusion
  77.9 0.5 convolution_subtract_fusion
  78.3 0.5 convolution_add_fusion
  78.8 0.0 copy-start.7
  78.8 0.0 copy-start.2
  78.8 0.0 copy-start.1
  78.8 1.1 pad_maximum_fusion.1
  79.9 5.8 %all-to-all-start = ((f32[2,8,64,256]{3,2,0,1:T(8,128)}), f32[2,8,64,256]{3,2,0,1:T(8,128)S(1)}, u32[]{:S(2)}, u32[]{:S(2)}) async-start(f32[2,8,64,256]{3,2,0,1:T(8,128)} %pad_maximum_fusion.1), calls=%async_computation | async-start | bytes 2097152 | tf_op jit(solution)/shard_map/all_to_all | solution.py:50
  85.7 0.0 all-reduce.2.cloned.1.call-start
  85.7 0.0 copy-done.7
  85.7 0.6 fusion.52
  86.3 0.6 compare_convert_fusion
  86.9 0.0 copy-done.2
  86.9 0.0 copy-done.1
  87.0 0.1 multiply_reduce_fusion
  87.1 24.5 %all-to-all-done = f32[2,8,64,256]{3,2,0,1:T(8,128)S(1)} async-done(((f32[2,8,64,256]{3,2,0,1:T(8,128)}), f32[2,8,64,256]{3,2,0,1:T(8,128)S(1)}, u32[]{:S(2)}, u32[]{:S(2)}) %all-to-all-start) | async-done | bytes 1048608 | tf_op jit(solution)/shard_map/all_to_all | solution.py:50
  111.6 0.8 copy.17
  112.4 2.6 %gather_fusion.1 = f32[512,2,256]{2,1,0:T(2,128)S(1)} fusion(f32[2,512,256]{2,0,1:T(2,128)S(1)} %bitcast.83, s32[1024]{0:T(1024)S(1)} %pad_clamp_fusion), kind=kCustom, calls=%fused_computation.1 | custom fusion | bytes 2099200 | tf_op jit(solution)/shard_map/jit(_take)/gather | solution.py:57
  115.0 0.2 fusion.31
  115.2 0.1 multiply_subtract_fusion
  115.3 1.0 pad_maximum_fusion.2
  116.3 0.0 all-reduce.2.cloned.1.call-update
  116.3 18.6 %all-reduce.2.cloned.1.call-done = f32[2,512,256]{2,1,0:T(8,128)} async-done(((f32[2,512,256]{2,1,0:T(8,128)}), f32[2,512,256]{2,1,0:T(8,128)}) %all-reduce.2.cloned.1.call-update) | async-done | bytes 1048592 | tf_op jit(solution)/shard_map/psum | solution.py:64
  135.0 2.3 %copy.23 = f32[2,512,256]{2,1,0:T(8,128)} copy(f32[2,512,256]{2,1,0:T(8,128)} %all-reduce.2.cloned.1.call-done) | data formatting | bytes 2097152
  (8 shorter events, 0.0 us)
Async XLA Ops:
  6.5 4.6 %copy-start.4 = (bf16[2,1024,1024]{2,1,0:T(8,128)(2,1)S(1)}, bf16[2,1024,1024]{2,1,0:T(8,128)(2,1)}, u32[]{:S(2)}) copy-start(bf16[2,1024,1024]{2,1,0:T(8,128)(2,1)} %param.11) | copy-start | bytes 12582916
  6.5 4.6 %copy-start.6 = (bf16[1,2,512,1024]{3,2,1,0:T(8,128)(2,1)S(1)}, bf16[1,2,512,1024]{3,2,1,0:T(8,128)(2,1)}, u32[]{:S(2)}) copy-start(bf16[1,2,512,1024]{3,2,1,0:T(8,128)(2,1)} %param.8) | copy-start | bytes 6291460
  13.8 3.6 %copy-start.5 = (bf16[2,1024,1024]{2,1,0:T(8,128)(2,1)S(1)}, bf16[2,1024,1024]{2,1,0:T(8,128)(2,1)}, u32[]{:S(2)}) copy-start(bf16[2,1024,1024]{2,1,0:T(8,128)(2,1)} %param.11) | copy-start | bytes 12582916
  13.8 4.1 %copy-start.8 = (f32[512,1024]{1,0:T(8,128)S(1)}, f32[512,1024]{1,0:T(8,128)}, u32[]{:S(2)}) copy-start(f32[512,1024]{1,0:T(8,128)} %fusion) | copy-start | bytes 6291460
  19.2 4.6 %copy-start.3 = (s32[1024]{0:T(1024)S(1)}, s32[1024]{0:T(1024)}, u32[]{:S(2)}) copy-start(s32[1024]{0:T(1024)} %param.10) | copy-start | bytes 12292
  19.7 49.9 %collective-permute-start = (bf16[2,512,512]{2,1,0:T(8,128)(2,1)S(1)}, bf16[2,512,512]{2,1,0:T(8,128)(2,1)}, u32[]{:S(2)}, u32[]{:S(2)}) collective-permute-start(bf16[2,512,512]{2,1,0:T(8,128)(2,1)S(1)} %get-tuple-element.5), channel_id=1, source_target_pairs={{0,8},{2,10},{4,12},{6,14},{8,0},{10,2},{12,4},{14,6},{1,9},{3,11}... | collective-permute-start | bytes 3145736 | tf_op jit(solution)/shard_map/ppermute | solution.py:10
  74.3 1.3 copy-start
  78.8 6.9 %copy-start.7 = (s32[1,4]{1,0:T(1,128)S(1)}, s32[1,4]{1,0:T(1,128)}, u32[]{:S(2)}) copy-start(s32[1,4]{1,0:T(1,128)} %param.9) | copy-start | bytes 52
  78.8 8.1 %copy-start.2 = (s32[512]{0:T(512)S(1)}, s32[512]{0:T(512)}, u32[]{:S(2)}) copy-start(s32[512]{0:T(512)} %param.15) | copy-start | bytes 6148
  78.8 8.1 %copy-start.1 = (f32[16,2,256]{2,1,0:T(2,128)S(1)}, f32[16,2,256]{2,1,0:T(2,128)}, u32[]{:S(2)}) copy-start(f32[16,2,256]{2,1,0:T(2,128)} %param.14) | copy-start | bytes 98308
  79.9 31.7 %all-to-all-start = ((f32[2,8,64,256]{3,2,0,1:T(8,128)}), f32[2,8,64,256]{3,2,0,1:T(8,128)S(1)}, u32[]{:S(2)}, u32[]{:S(2)}) async-start(f32[2,8,64,256]{3,2,0,1:T(8,128)} %pad_maximum_fusion.1), calls=%async_computation | async-start | bytes 2097152 | tf_op jit(solution)/shard_map/all_to_all | solution.py:50
  85.7 49.3 %all-reduce.2.cloned.1.call-start = ((), (), s32[]{:S(2)}) async-start(), calls=%async_computation.1 | async-start | bytes 2097152 | tf_op jit(solution)/shard_map/psum | solution.py:64
Sparse Core Ops, SparseCore 0:
  116.5 18.4 all-reduce.1
where the time goes:
time: 145 us; the launch traced here: 144 us
  waiting for transfers between devices  54.1 us (37%)
  local copies, waits for them, and re-layouts  38.3 us (26%)
  matrix products  19.1 us (13%)
  between operations  13.7 us (9%)
  starting transfers between devices  9.93 us (7%)
  other arithmetic  9.01 us (6%)
    gather x1, local copies, waits for them, and re-layouts, on_device(): reordered = jnp.take(branch_second, inverse, axis=1)  27.6 us
    all_to_all x1, waiting for transfers between devices, on_device(): lax.all_to_all(contracted.reshape(2, stem_size, block_rows, contracted.sh...  24.5 us
    psum x1, waiting for transfers between devices, on_device(): return lax.psum(total, 'cuts')  18.6 us
    ppermute x1, waiting for transfers between devices, swapped(): return lax.ppermute(value, axis, pairs)  10.9 us
    dot_general x3, matrix products, complex_dot(): jnp.dot(operand[1], matrix[1], preferred_element_type=jnp.float32)  6.33 us
    all_to_all x1, starting transfers between devices, on_device(): lax.all_to_all(contracted.reshape(2, stem_size, block_rows, contracted.sh...  5.77 us
    dot_general x3, matrix products, complex_dot(): jnp.dot(operand[0], matrix[0], preferred_element_type=jnp.float32)  5.36 us
    scatter x1, local copies, waits for them, and re-layouts, on_device(): jnp.zeros_like(index_order).at[index_order]  4.49 us
  transfers between devices with their start and end apart: 3, of which 3 were waited for; matrix products, arithmetic and copies ran while one was open for 25% of the time, Pallas kernels for 0%

commit v1 on v0

--- a/solution.py
+++ b/solution.py
@@ -47,13 +47,19 @@
     )
     second = complex_dot(joined, reordered).astype(jnp.bfloat16)
     contracted = complex_dot(second, branch_third)
-    moved = lax.all_to_all(
-        contracted.reshape(2, stem_size, block_rows, contracted.shape[2]),
-        "stem",
-        split_axis=1,
-        concat_axis=1,
-        tiled=True,
-    )
+    x = contracted.reshape(2, stem_size, block_rows, contracted.shape[2])
+    ways, here = (lax.axis_size("stem"), lax.axis_index("stem"))
+    width_2 = x.shape[1] // ways
+    shape = list(x.shape)
+    shape[1] = width_2
+    height = shape[1]
+    shape[1] = height * ways
+    moved = jnp.zeros(shape, x.dtype)
+    for mask_2 in range(ways):
+        part = lax.dynamic_slice_in_dim(x, (here ^ mask_2) * width_2, width_2, axis=1)
+        if mask_2:
+            part = lax.ppermute(part, "stem", [(d, d ^ mask_2) for d in range(ways)])
+        moved = lax.dynamic_update_slice_in_dim(moved, part, (here ^ mask_2) * height, axis=1)
     third = jnp.take(moved.reshape(2, rows_dev, contracted.shape[2]), picks, axis=1)
     code = jnp.sum(edge_values[0] * powers)
     onehot = (codes == code).astype(jnp.float32)

time: 145 us -> 138 us (0.952)
  waiting for transfers between devices: 54.1 us -> 39.4 us
  starting transfers between devices: 9.93 us -> 18 us
    all_to_all x1 -> x0, waiting for transfers between devices: 24.5 us -> none  [on_device(): lax.all_to_all(contracted.reshape(2, stem_size, block_rows, contracted.sh...]
    ppermute x0 -> x7, starting transfers between devices: none -> 13.9 us  [on_device(): part = lax.ppermute(part, 'stem', [(d, d ^ mask_2) for d in range(ways)])]
    ppermute x0 -> x7, waiting for transfers between devices: none -> 7.35 us  [on_device(): part = lax.ppermute(part, 'stem', [(d, d ^ mask_2) for d in range(ways)])]
    all_to_all x1 -> x0, starting transfers between devices: 5.77 us -> none  [on_device(): lax.all_to_all(contracted.reshape(2, stem_size, block_rows, contracted.sh...]
    psum x1, waiting for transfers between devices: 18.6 us -> 22.8 us  [on_device(): return lax.psum(total, 'cuts')]
    ppermute x1, waiting for transfers between devices: 10.9 us -> 9.26 us  [swapped(): return lax.ppermute(value, axis, pairs)]
  transfers between devices with their start and end apart: 3 -> 9, of which waited for: 3 -> 6; matrix products, arithmetic and copies ran while one was open for 25% -> 27% of each run, Pallas kernels for 0% -> 0%
where the time goes in v1:
time: 138 us; the launch traced here: 137 us
  waiting for transfers between devices  39.4 us (29%)
  local copies, waits for them, and re-layouts  38.8 us (28%)
  matrix products  19.1 us (14%)
  starting transfers between devices  18 us (13%)
  between operations  13.7 us (10%)
  other arithmetic  8.01 us (6%)
    gather x1, local copies, waits for them, and re-layouts, on_device(): reordered = jnp.take(branch_second, inverse, axis=1)  27.8 us
    psum x1, waiting for transfers between devices, on_device(): return lax.psum(total, 'cuts')  22.8 us
    ppermute x7, starting transfers between devices, on_device(): part = lax.ppermute(part, 'stem', [(d, d ^ mask_2) for d in range(ways)])  13.9 us
    ppermute x1, waiting for transfers between devices, swapped(): return lax.ppermute(value, axis, pairs)  9.26 us
    ppermute x7, waiting for transfers between devices, on_device(): part = lax.ppermute(part, 'stem', [(d, d ^ mask_2) for d in range(ways)])  7.35 us
    dot_general x3, matrix products, complex_dot(): jnp.dot(operand[1], matrix[1], preferred_element_type=jnp.float32)  6.35 us
    dot_general x3, matrix products, complex_dot(): jnp.dot(operand[0], matrix[0], preferred_element_type=jnp.float32)  5.39 us
    scatter x1, local copies, waits for them, and re-layouts, on_device(): jnp.zeros_like(index_order).at[index_order]  4.49 us
  transfers between devices with their start and end apart: 9, of which 6 were waited for; matrix products, arithmetic and copies ran while one was open for 27% of the time, Pallas kernels for 0%

profile of v1, /device:TPU:0, one launch (start us, length us, event | category | flops | bytes accessed | tf_op | source)
XLA Modules:
  0.0 137.1 jit_solution(10652034518276904812)
XLA Ops:
  6.5 0.0 all-reduce.2.cloned.1.call-start
  6.5 4.6 %fusion.2 = f32[512,1024]{1,0:T(8,128)} fusion(bf16[2,1024,1024]{2,1,0:T(8,128)(2,1)} %param.11, bf16[1,2,512,1024]{3,2,1,0:T(8,128)(2,1)} %param.8), kind=kOutput, calls=%fused_computation.27 | convolution fusion | flops 1073741824 | bytes 5242880 | tf_op jit(solution)/shard_map/dot_general | solution.py:14
  11.2 0.0 copy-done.4
  11.2 0.0 copy-done.6
  11.2 2.6 %fusion = f32[512,1024]{1,0:T(8,128)} fusion(bf16[2,1024,1024]{2,1,0:T(8,128)(2,1)S(1)} %copy-done.4, bf16[1,2,512,1024]{3,2,1,0:T(8,128)(2,1)S(1)} %copy-done.6), kind=kOutput, calls=%fused_computation.25 | convolution fusion | flops 1073741824 | bytes 5242880 | tf_op jit(solution)/shard_map/dot_general | solution.py:17
  13.8 3.6 %fusion.20 = bf16[1,512,1024]{2,1,0:T(8,128)(2,1)S(1)} fusion(f32[512,1024]{1,0:T(8,128)} %fusion.2, bf16[2,1024,1024]{2,1,0:T(8,128)(2,1)} %param.11, bf16[1,2,512,1024]{3,2,1,0:T(8,128)(2,1)S(1)} %copy-done.6), kind=kOutput, calls=%fused_computation.45 | convolution fusion | flops 1074790400 | bytes 6291456 | tf_op jit(solution)/shard_map/dot_general | solution.py:14
  17.4 0.0 copy-done.5
  17.5 0.5 copy-done.8
  17.9 1.3 fusion.23
  19.2 0.0 copy-start.2
  19.2 0.0 copy-start.3
  19.2 0.0 copy-start.7
  19.2 0.4 broadcast_select_fusion
  19.7 4.1 %collective-permute-start = (bf16[2,512,512]{2,1,0:T(8,128)(2,1)S(1)}, bf16[2,512,512]{2,1,0:T(8,128)(2,1)}, u32[]{:S(2)}, u32[]{:S(2)}) collective-permute-start(bf16[2,512,512]{2,1,0:T(8,128)(2,1)S(1)} %get-tuple-element.5), channel_id=1, source_target_pairs={{0,8},{2,10},{4,12},{6,14},{8,0},{10,2},{12,4},{14,6},{1,9},{3,11}... | collective-permute-start | bytes 3145736 | tf_op jit(solution)/shard_map/ppermute | solution.py:10
  23.9 4.5 %scatter_custom_fusion = s32[1024]{0:T(1024)S(1)} fusion(s32[1024]{0:T(1024)S(1)} %compare_select_fusion.1, s32[1024]{0:T(1024)S(1)} %iota.11, s32[]{:T(128)} %constant.46.clone.1), kind=kCustom, calls=%fused_computation.100 | custom fusion | bytes 4100 | tf_op jit(solution)/shard_map/scatter | solution.py:34
  28.4 0.6 fusion.60
  29.0 0.6 compare_convert_fusion
  29.7 0.0 copy-start.1
  29.7 27.8 %gather_fusion = bf16[1024,2,1024]{2,0,1:T(8,128)(2,1)} fusion(bf16[2,1024,1024]{2,1,0:T(8,128)(2,1)} %param.12, s32[1024]{0:T(1024)S(1)} %fusion.54), kind=kCustom, calls=%fused_computation | custom fusion | bytes 8392704 | tf_op jit(solution)/shard_map/jit(_take)/gather | solution.py:35
  57.5 0.1 multiply_reduce_fusion
  57.7 2.6 %select_bitcast_fusion = bf16[2,1024,1024]{2,1,0:T(8,128)(2,1)S(1)} fusion(bf16[1024,2,1024]{2,0,1:T(8,128)(2,1)} %gather_fusion, pred[1024]{0:T(1024)(128)(4,1)S(1)} %compare_and_fusion), kind=kLoop, calls=%fused_computation.3 | loop fusion | flops 2097152 | bytes 8389632 | tf_op jit(solution)/shard_map/jit(_take)/select_n | solution.py:35
  60.3 9.3 %collective-permute-done = bf16[2,512,512]{2,1,0:T(8,128)(2,1)} collective-permute-done((bf16[2,512,512]{2,1,0:T(8,128)(2,1)S(1)}, bf16[2,512,512]{2,1,0:T(8,128)(2,1)}, u32[]{:S(2)}, u32[]{:S(2)}) %collective-permute-start) | collective-permute-done | bytes 1048608 | tf_op jit(solution)/shard_map/ppermute | solution.py:10
  69.6 2.1 %maximum_select_fusion = bf16[2,512,1024]{2,1,0:T(8,128)(2,1)S(1)} fusion(bf16[2,512,512]{2,1,0:T(8,128)(2,1)} %collective-permute-done, bf16[2,512,512]{2,1,0:T(8,128)(2,1)S(1)} %get-tuple-element.6, bf16[2,512,512]{2,1,0:T(8,128)(2,1)S(1)} %get-tuple-element.7, pred[]{:T(512)S(6)} %eq.15), kind=kLoop, calls=%fused_computation.24 | loop fusion | flops 9437184 | bytes 5242881 | tf_op jit(solution)/shard_map/jit(_where)/select_n | solution.py:43
  71.7 1.3 fusion.8
  73.0 1.3 fusion.11
  74.2 0.0 copy-start
  74.2 1.3 subtract_convert_fusion
  75.5 0.0 copy-done
  75.5 0.5 fusion.36
  76.0 0.5 fusion.40
  76.5 1.3 add_convert_fusion
  77.8 0.5 convolution_add_fusion
  78.2 0.5 convolution_subtract_fusion
  78.7 0.5 collective-permute-start.5
  79.2 0.1 fusion.46
  79.3 1.2 collective-permute-start.1
  80.5 4.0 %collective-permute-start.2 = (f32[2,1,64,256]{3,2,1,0:T(8,128)S(1)}, f32[2,1,64,256]{3,2,1,0:T(8,128)S(1)}, u32[]{:S(2)}, u32[]{:S(2)}) collective-permute-start(f32[2,1,64,256]{3,2,1,0:T(8,128)S(1)} %get-tuple-element.13), channel_id=1, source_target_pairs={{0,4},{2,6},{4,0},{6,2},{8,12},{10,14},{12,8},{14,10},{1,5},{3,7},... | collective-permute-start | bytes 393224 | tf_op jit(solution)/shard_map/ppermute | solution.py:61
  84.5 1.0 collective-permute-start.3
  85.4 0.9 collective-permute-start.4
  86.3 0.3 broadcast_in_dim.36
  86.6 0.1 copy_dynamic-update-slice_fusion.7
  86.7 0.0 collective-permute-done.1
  86.7 4.1 %collective-permute-start.6 = (f32[2,1,64,256]{3,2,1,0:T(8,128)S(1)}, f32[2,1,64,256]{3,2,1,0:T(8,128)S(1)}, u32[]{:S(2)}, u32[]{:S(2)}) collective-permute-start(f32[2,1,64,256]{3,2,1,0:T(8,128)S(1)} %get-tuple-element.16), channel_id=1, source_target_pairs={{0,12},{2,14},{4,8},{6,10},{8,4},{10,6},{12,0},{14,2},{1,13},{3,15... | collective-permute-start | bytes 393224 | tf_op jit(solution)/shard_map/ppermute | solution.py:61
  90.8 0.1 copy_dynamic-update-slice_fusion.6
  90.9 2.1 %collective-permute-done.2 = f32[2,1,64,256]{3,2,1,0:T(8,128)S(1)} collective-permute-done((f32[2,1,64,256]{3,2,1,0:T(8,128)S(1)}, f32[2,1,64,256]{3,2,1,0:T(8,128)S(1)}, u32[]{:S(2)}, u32[]{:S(2)}) %collective-permute-start.2) | collective-permute-done | bytes 131104 | tf_op jit(solution)/shard_map/ppermute | solution.py:61
  93.0 2.3 %collective-permute-start.7 = (f32[2,1,64,256]{3,2,1,0:T(8,128)S(1)}, f32[2,1,64,256]{3,2,1,0:T(8,128)S(1)}, u32[]{:S(2)}, u32[]{:S(2)}) collective-permute-start(f32[2,1,64,256]{3,2,1,0:T(8,128)S(1)} %get-tuple-element.10), channel_id=1, source_target_pairs={{0,14},{2,12},{4,10},{6,8},{8,6},{10,4},{12,2},{14,0},{1,15},{3,13... | collective-permute-start | bytes 393224 | tf_op jit(solution)/shard_map/ppermute | solution.py:61
  95.2 0.1 copy_dynamic-update-slice_fusion.5
  95.4 0.7 collective-permute-done.3
  96.1 0.1 copy_dynamic-update-slice_fusion.4
  96.2 0.0 collective-permute-done.4
  96.2 0.1 copy_dynamic-update-slice_fusion.3
  96.3 0.0 collective-permute-done.5
  96.3 0.1 copy_dynamic-update-slice_fusion.2
  96.5 2.1 %collective-permute-done.6 = f32[2,1,64,256]{3,2,1,0:T(8,128)S(1)} collective-permute-done((f32[2,1,64,256]{3,2,1,0:T(8,128)S(1)}, f32[2,1,64,256]{3,2,1,0:T(8,128)S(1)}, u32[]{:S(2)}, u32[]{:S(2)}) %collective-permute-start.6) | collective-permute-done | bytes 131104 | tf_op jit(solution)/shard_map/ppermute | solution.py:61
  98.5 0.1 copy_dynamic-update-slice_fusion.1
  98.6 2.5 %collective-permute-done.7 = f32[2,1,64,256]{3,2,1,0:T(8,128)S(1)} collective-permute-done((f32[2,1,64,256]{3,2,1,0:T(8,128)S(1)}, f32[2,1,64,256]{3,2,1,0:T(8,128)S(1)}, u32[]{:S(2)}, u32[]{:S(2)}) %collective-permute-start.7) | collective-permute-done | bytes 131104 | tf_op jit(solution)/shard_map/ppermute | solution.py:61
  101.1 0.1 copy_dynamic-update-slice_fusion
  101.2 2.6 %gather_fusion.1 = f32[512,2,256]{2,1,0:T(2,128)S(1)} fusion(f32[2,512,256]{2,0,1:T(2,128)S(1)} %bitcast.83, s32[1024]{0:T(1024)S(1)} %pad_clamp_fusion), kind=kCustom, calls=%fused_computation.1 | custom fusion | bytes 2099200 | tf_op jit(solution)/shard_map/jit(_take)/gather | solution.py:63
  103.8 0.2 fusion.31
  104.0 0.1 multiply_subtract_fusion
  104.1 1.0 pad_maximum_fusion.1
  105.2 0.0 all-reduce.2.cloned.1.call-update
  105.2 22.8 %all-reduce.2.cloned.1.call-done = f32[2,512,256]{2,1,0:T(8,128)} async-done(((f32[2,512,256]{2,1,0:T(8,128)}), f32[2,512,256]{2,1,0:T(8,128)}) %all-reduce.2.cloned.1.call-update) | async-done | bytes 1048592 | tf_op jit(solution)/shard_map/psum | solution.py:70
  128.0 2.3 %copy.47 = f32[2,512,256]{2,1,0:T(8,128)} copy(f32[2,512,256]{2,1,0:T(8,128)} %all-reduce.2.cloned.1.call-done) | data formatting | bytes 2097152
  (17 shorter events, 0.1 us)
Async XLA Ops:
  6.5 121.5 %all-reduce.2.cloned.1.call-start = ((), (), s32[]{:S(2)}) async-start(), calls=%async_computation | async-start | bytes 2097152 | tf_op jit(solution)/shard_map/psum | solution.py:70
  6.5 4.6 %copy-start.4 = (bf16[2,1024,1024]{2,1,0:T(8,128)(2,1)S(1)}, bf16[2,1024,1024]{2,1,0:T(8,128)(2,1)}, u32[]{:S(2)}) copy-start(bf16[2,1024,1024]{2,1,0:T(8,128)(2,1)} %param.11) | copy-start | bytes 12582916
  6.5 4.6 %copy-start.6 = (bf16[1,2,512,1024]{3,2,1,0:T(8,128)(2,1)S(1)}, bf16[1,2,512,1024]{3,2,1,0:T(8,128)(2,1)}, u32[]{:S(2)}) copy-start(bf16[1,2,512,1024]{3,2,1,0:T(8,128)(2,1)} %param.8) | copy-start | bytes 6291460
  13.8 3.7 %copy-start.5 = (bf16[2,1024,1024]{2,1,0:T(8,128)(2,1)S(1)}, bf16[2,1024,1024]{2,1,0:T(8,128)(2,1)}, u32[]{:S(2)}) copy-start(bf16[2,1024,1024]{2,1,0:T(8,128)(2,1)} %param.11) | copy-start | bytes 12582916
  13.8 4.1 %copy-start.8 = (f32[512,1024]{1,0:T(8,128)S(1)}, f32[512,1024]{1,0:T(8,128)}, u32[]{:S(2)}) copy-start(f32[512,1024]{1,0:T(8,128)} %fusion) | copy-start | bytes 6291460
  19.2 4.6 %copy-start.2 = (s32[512]{0:T(512)S(1)}, s32[512]{0:T(512)}, u32[]{:S(2)}) copy-start(s32[512]{0:T(512)} %param.15) | copy-start | bytes 6148
  19.2 4.6 %copy-start.3 = (s32[1024]{0:T(1024)S(1)}, s32[1024]{0:T(1024)}, u32[]{:S(2)}) copy-start(s32[1024]{0:T(1024)} %param.10) | copy-start | bytes 12292
  19.2 9.2 %copy-start.7 = (s32[1,4]{1,0:T(1,128)S(1)}, s32[1,4]{1,0:T(1,128)}, u32[]{:S(2)}) copy-start(s32[1,4]{1,0:T(1,128)} %param.9) | copy-start | bytes 52
  19.7 49.9 %collective-permute-start = (bf16[2,512,512]{2,1,0:T(8,128)(2,1)S(1)}, bf16[2,512,512]{2,1,0:T(8,128)(2,1)}, u32[]{:S(2)}, u32[]{:S(2)}) collective-permute-start(bf16[2,512,512]{2,1,0:T(8,128)(2,1)S(1)} %get-tuple-element.5), channel_id=1, source_target_pairs={{0,8},{2,10},{4,12},{6,14},{8,0},{10,2},{12,4},{14,6},{1,9},{3,11}... | collective-permute-start | bytes 3145736 | tf_op jit(solution)/shard_map/ppermute | solution.py:10
  29.7 27.8 %copy-start.1 = (f32[16,2,256]{2,1,0:T(2,128)S(1)}, f32[16,2,256]{2,1,0:T(2,128)}, u32[]{:S(2)}) copy-start(f32[16,2,256]{2,1,0:T(2,128)} %param.14) | copy-start | bytes 98308
  74.2 1.3 copy-start
  78.7 17.6 %collective-permute-start.5 = (f32[2,1,64,256]{3,2,1,0:T(8,128)S(1)}, f32[2,1,64,256]{3,2,1,0:T(8,128)S(1)}, u32[]{:S(2)}, u32[]{:S(2)}) collective-permute-start(f32[2,1,64,256]{3,2,1,0:T(8,128)S(1)} %get-tuple-element.17), channel_id=1, source_target_pairs={{0,10},{2,8},{4,14},{6,12},{8,2},{10,0},{12,6},{14,4},{1,11},{3,9}... | collective-permute-start | bytes 393224 | tf_op jit(solution)/shard_map/ppermute | solution.py:61
  79.3 7.4 %collective-permute-start.1 = (f32[2,1,64,256]{3,2,1,0:T(8,128)S(1)}, f32[2,1,64,256]{3,2,1,0:T(8,128)S(1)}, u32[]{:S(2)}, u32[]{:S(2)}) collective-permute-start(f32[2,1,64,256]{3,2,1,0:T(8,128)S(1)} %get-tuple-element.12), channel_id=1, source_target_pairs={{0,2},{2,0},{4,6},{6,4},{8,10},{10,8},{12,14},{14,12},{1,3},{3,1},... | collective-permute-start | bytes 393224 | tf_op jit(solution)/shard_map/ppermute | solution.py:61
  80.5 12.5 %collective-permute-start.2 = (f32[2,1,64,256]{3,2,1,0:T(8,128)S(1)}, f32[2,1,64,256]{3,2,1,0:T(8,128)S(1)}, u32[]{:S(2)}, u32[]{:S(2)}) collective-permute-start(f32[2,1,64,256]{3,2,1,0:T(8,128)S(1)} %get-tuple-element.13), channel_id=1, source_target_pairs={{0,4},{2,6},{4,0},{6,2},{8,12},{10,14},{12,8},{14,10},{1,5},{3,7},... | collective-permute-start | bytes 393224 | tf_op jit(solution)/shard_map/ppermute | solution.py:61
  84.5 11.6 %collective-permute-start.3 = (f32[2,1,64,256]{3,2,1,0:T(8,128)S(1)}, f32[2,1,64,256]{3,2,1,0:T(8,128)S(1)}, u32[]{:S(2)}, u32[]{:S(2)}) collective-permute-start(f32[2,1,64,256]{3,2,1,0:T(8,128)S(1)} %get-tuple-element.14), channel_id=1, source_target_pairs={{0,6},{2,4},{4,2},{6,0},{8,14},{10,12},{12,10},{14,8},{1,7},{3,5},... | collective-permute-start | bytes 393224 | tf_op jit(solution)/shard_map/ppermute | solution.py:61
  85.4 10.8 %collective-permute-start.4 = (f32[2,1,64,256]{3,2,1,0:T(8,128)S(1)}, f32[2,1,64,256]{3,2,1,0:T(8,128)S(1)}, u32[]{:S(2)}, u32[]{:S(2)}) collective-permute-start(f32[2,1,64,256]{3,2,1,0:T(8,128)S(1)} %get-tuple-element.15), channel_id=1, source_target_pairs={{0,8},{2,10},{4,12},{6,14},{8,0},{10,2},{12,4},{14,6},{1,9},{3,11}... | collective-permute-start | bytes 393224 | tf_op jit(solution)/shard_map/ppermute | solution.py:61
  86.7 11.8 %collective-permute-start.6 = (f32[2,1,64,256]{3,2,1,0:T(8,128)S(1)}, f32[2,1,64,256]{3,2,1,0:T(8,128)S(1)}, u32[]{:S(2)}, u32[]{:S(2)}) collective-permute-start(f32[2,1,64,256]{3,2,1,0:T(8,128)S(1)} %get-tuple-element.16), channel_id=1, source_target_pairs={{0,12},{2,14},{4,8},{6,10},{8,4},{10,6},{12,0},{14,2},{1,13},{3,15... | collective-permute-start | bytes 393224 | tf_op jit(solution)/shard_map/ppermute | solution.py:61
  93.0 8.2 %collective-permute-start.7 = (f32[2,1,64,256]{3,2,1,0:T(8,128)S(1)}, f32[2,1,64,256]{3,2,1,0:T(8,128)S(1)}, u32[]{:S(2)}, u32[]{:S(2)}) collective-permute-start(f32[2,1,64,256]{3,2,1,0:T(8,128)S(1)} %get-tuple-element.10), channel_id=1, source_target_pairs={{0,14},{2,12},{4,10},{6,8},{8,6},{10,4},{12,2},{14,0},{1,15},{3,13... | collective-permute-start | bytes 393224 | tf_op jit(solution)/shard_map/ppermute | solution.py:61
Sparse Core Ops, SparseCore 0:
  105.3 22.6 all-reduce.1
